TPU v7x, 32 devices: a whole 2x2x4 slice. The times are simulated.
32 devices in a mesh: shard: 8 (over z, x), seq: 4 (over y, core).
Axes of the slice: x: 2, y: 2, z: 4, core: 2. Of those that a mesh axis runs over, the one named last changes fastest.
Arguments:
- inputs: bfloat16 [16, 512, 768], P('shard', 'seq'), may hold values from -6 to 6
- lengths: int32 [16], P('shard'), may hold values from 128 to 512, as said below
- w_query: bfloat16 [768, 768], P('shard'), may hold values from -0.21875 to 0.21875
- b_query: bfloat16 [768], P('shard'), may hold values from -3 to 3
- w_key: bfloat16 [768, 768], P('shard'), may hold values from -0.21875 to 0.21875
- w_value: bfloat16 [768, 768], P('shard'), may hold values from -0.21875 to 0.21875
- b_value: bfloat16 [768], P('shard'), may hold values from -2 to 2
- w_output: bfloat16 [768, 768], P('shard'), may hold values from -0.875 to 0.875
- b_output: bfloat16 [768], P('shard'), may hold values from -2 to 2
- gain_one: bfloat16 [768], P('shard'), may hold values from 0.25 to 1.75
- shift_one: bfloat16 [768], P('shard'), may hold values from -2 to 2
- w_inner: bfloat16 [768, 3072], P('shard'), may hold values from -0.21875 to 0.21875
- b_inner: bfloat16 [3072], P('shard'), may hold values from -2 to 2
- w_outer: bfloat16 [3072, 768], P('shard'), may hold values from -0.109375 to 0.109375
- b_outer: bfloat16 [768], P('shard'), may hold values from -2 to 2
- gain_two: bfloat16 [768], P('shard'), may hold values from 0.25 to 1.75
- shift_two: bfloat16 [768], P('shard'), may hold values from -2 to 2
- cotangent: bfloat16 [16, 512, 768], P('shard', 'seq'), may hold values from -6 to 6
Outputs:
- output: bfloat16 [16, 512, 768], P('shard', 'seq')
- grad_inputs: float32 [16, 512, 768], P('shard', 'seq')
- grad_w_query: float32 [768, 768], P('shard')
- grad_b_query: float32 [768], P('shard')
- grad_w_key: float32 [768, 768], P('shard')
- grad_w_value: float32 [768, 768], P('shard')
- grad_b_value: float32 [768], P('shard')
- grad_w_output: float32 [768, 768], P('shard')
- grad_b_output: float32 [768], P('shard')
- grad_gain_one: float32 [768], P('shard')
- grad_shift_one: float32 [768], P('shard')
- grad_w_inner: float32 [768, 3072], P('shard')
- grad_b_inner: float32 [3072], P('shard')
- grad_w_outer: float32 [3072, 768], P('shard')
- grad_b_outer: float32 [768], P('shard')
- grad_gain_two: float32 [768], P('shard')
- grad_shift_two: float32 [768], P('shard')
Inputs may be any that keep to these rules, and one draw needn't show every extreme that they name: `lengths`: every draw has a slot of 512 valid tokens and a slot of 128.
All inputs are finite; a program needn't handle non-finite values.
Results may differ from a plain program's by a relative error of at most 0.017.
Values may be sent and summed in bfloat16 or wider, within the bound.
A program may use at most 128 MiB of HBM per device.

v0:
```python
from functools import partial
import jax
import jax.numpy as jnp
from jax import lax
from jax.sharding import PartitionSpec as P

HEAD_DIM = 64
epsilon = 1e-12


def layer_norm(tensor, norm_gain, norm_shift):
    average = jnp.mean(tensor, axis=-1, keepdims=True)
    centred = tensor - average
    variance = jnp.mean(centred * centred, axis=-1, keepdims=True)
    return centred * lax.rsqrt(variance + epsilon) * norm_gain + norm_shift


def product(operand, weight):
    return jnp.dot(operand, weight, preferred_element_type=jnp.float32)


def row_contract(operand, weight):
    return lax.dot_general(
        operand, weight, (((0,), (0,)), ((), ())), preferred_element_type=jnp.float32
    )


def times_transposed(operand, weight):
    return lax.dot_general(
        operand, weight, (((1,), (1,)), ((), ())), preferred_element_type=jnp.float32
    )


def column_sum(tensor):
    return jnp.sum(tensor.astype(jnp.float32), axis=0)


def head_logits(query_seq, key_seq, length, factor):
    scores = (
        jnp.einsum("qhd,khd->hqk", query_seq, key_seq, preferred_element_type=jnp.float32) * factor
    )
    visible = jnp.arange(key_seq.shape[0]) < length
    return jnp.where(visible[None, None, :], scores, -1000000000.0)


def per_device(
    inputs,
    lengths,
    w_query,
    b_query,
    w_key,
    w_value,
    b_value,
    w_output,
    b_output,
    gain_one,
    shift_one,
    w_inner,
    b_inner,
    w_outer,
    b_outer,
    gain_two,
    shift_two,
    cotangent,
):
    local_seqs, tok_dev, model_width = inputs.shape
    groups = lax.axis_size("seq")
    head_width = model_width // groups
    local_heads = head_width // HEAD_DIM
    factor = HEAD_DIM ** (-0.5)
    gathered = (
        lax.all_gather(w_query, "shard", axis=0, tiled=True),
        lax.all_gather(b_query, "shard", axis=0, tiled=True),
        lax.all_gather(w_key, "shard", axis=0, tiled=True),
        lax.all_gather(w_value, "shard", axis=0, tiled=True),
        lax.all_gather(b_value, "shard", axis=0, tiled=True),
        lax.all_gather(w_output, "shard", axis=0, tiled=True),
        lax.all_gather(b_output, "shard", axis=0, tiled=True),
        lax.all_gather(gain_one, "shard", axis=0, tiled=True),
        lax.all_gather(shift_one, "shard", axis=0, tiled=True),
        lax.all_gather(w_inner, "shard", axis=0, tiled=True),
        lax.all_gather(b_inner, "shard", axis=0, tiled=True),
        lax.all_gather(w_outer, "shard", axis=0, tiled=True),
        lax.all_gather(b_outer, "shard", axis=0, tiled=True),
        lax.all_gather(gain_two, "shard", axis=0, tiled=True),
        lax.all_gather(shift_two, "shard", axis=0, tiled=True),
    )
    (
        query_w,
        query_b,
        key_w,
        value_w,
        value_b,
        output_w,
        output_b,
        gain_a,
        shift_a,
        inner_w,
        inner_b,
        outer_w,
        outer_b,
        gain_b,
        shift_b,
    ) = gathered
    gain_first = gain_a.astype(jnp.float32)
    shift_first = shift_a.astype(jnp.float32)
    gain_second = gain_b.astype(jnp.float32)
    shift_second = shift_b.astype(jnp.float32)
    flat_rows = inputs.reshape(local_seqs * tok_dev, model_width)
    queries = (product(flat_rows, query_w) + query_b.astype(jnp.float32)).astype(jnp.bfloat16)
    key_rows = product(flat_rows, key_w).astype(jnp.bfloat16)
    values = (product(flat_rows, value_w) + value_b.astype(jnp.float32)).astype(jnp.bfloat16)
    shape_seq = (local_seqs, tok_dev, model_width)
    head_q, head_k, head_v = (
        lax.all_to_all(queries.reshape(shape_seq), "seq", split_axis=2, concat_axis=1, tiled=True),
        lax.all_to_all(key_rows.reshape(shape_seq), "seq", split_axis=2, concat_axis=1, tiled=True),
        lax.all_to_all(values.reshape(shape_seq), "seq", split_axis=2, concat_axis=1, tiled=True),
    )
    seq_len = head_q.shape[1]
    split = (local_seqs, seq_len, local_heads, HEAD_DIM)
    head_q = head_q.reshape(split)
    head_k = head_k.reshape(split)
    head_v = head_v.reshape(split)

    def attend(packed):
        query_seq, key_seq, value_seq, length = packed
        logits = head_logits(query_seq, key_seq, length, factor)
        row_max = jnp.max(logits, axis=-1, keepdims=True)
        shifted = jnp.exp(logits - row_max)
        row_total = jnp.sum(shifted, axis=-1, keepdims=True)
        weights = (shifted / row_total).astype(jnp.bfloat16)
        context = jnp.einsum("hqk,khd->qhd", weights, value_seq, preferred_element_type=jnp.float32)
        return (context.astype(jnp.bfloat16), (row_max + jnp.log(row_total))[..., 0])

    head_context, log_total = lax.map(attend, (head_q, head_k, head_v, lengths))
    back_shape = (local_seqs, seq_len, head_width)
    context = lax.all_to_all(
        head_context.reshape(back_shape), "seq", split_axis=1, concat_axis=2, tiled=True
    ).reshape(-1, model_width)
    branch = product(context, output_w) + output_b.astype(jnp.float32)
    summed = flat_rows.astype(jnp.float32) + branch
    normed = layer_norm(summed, gain_first, shift_first)
    normed_low = normed.astype(jnp.bfloat16)
    pre_inner = product(normed_low, inner_w) + inner_b.astype(jnp.float32)
    activated = jax.nn.gelu(pre_inner, approximate=False).astype(jnp.bfloat16)
    final_sum = normed + product(activated, outer_w) + outer_b.astype(jnp.float32)
    result = layer_norm(final_sum, gain_second, shift_second)
    grad_out = cotangent.reshape(-1, model_width).astype(jnp.float32)
    second_back = jax.vjp(layer_norm, final_sum, gain_second, shift_second)[1]
    grad_final, grad_gain_two, grad_shift_two = second_back(grad_out)
    grad_ffn = grad_final.astype(jnp.bfloat16)
    grad_w_outer = row_contract(activated, grad_ffn)
    grad_b_outer = column_sum(grad_ffn)
    grad_active = times_transposed(grad_ffn, outer_w)
    gelu_back = jax.vjp(partial(jax.nn.gelu, approximate=False), pre_inner)[1]
    grad_pre = gelu_back(grad_active)[0].astype(jnp.bfloat16)
    grad_w_inner = row_contract(normed_low, grad_pre)
    grad_b_inner = column_sum(grad_pre)
    grad_normed = grad_final + times_transposed(grad_pre, inner_w)
    first_back = jax.vjp(layer_norm, summed, gain_first, shift_first)[1]
    grad_summed, grad_gain_one, grad_shift_one = first_back(grad_normed)
    grad_branch = grad_summed.astype(jnp.bfloat16)
    grad_w_output = row_contract(context, grad_branch)
    grad_b_output = column_sum(grad_branch)
    grad_context = times_transposed(grad_branch, output_w).astype(jnp.bfloat16)
    grad_head_context = lax.all_to_all(
        grad_context.reshape(shape_seq), "seq", split_axis=2, concat_axis=1, tiled=True
    ).reshape(split)

    def attend_back(packed):
        query_seq, key_seq, value_seq, log_sum, grad_seq, length = packed
        logits = head_logits(query_seq, key_seq, length, factor)
        attn_probs = jnp.exp(logits - log_sum[..., None])
        weights = attn_probs.astype(jnp.bfloat16)
        grad_value = jnp.einsum(
            "hqk,qhd->khd", weights, grad_seq, preferred_element_type=jnp.float32
        )
        grad_probs = jnp.einsum(
            "qhd,khd->hqk", grad_seq, value_seq, preferred_element_type=jnp.float32
        )
        inner_sum = jnp.sum(grad_probs * attn_probs, axis=-1, keepdims=True)
        grad_scores = (attn_probs * (grad_probs - inner_sum)).astype(jnp.bfloat16)
        grad_query = (
            jnp.einsum("hqk,khd->qhd", grad_scores, key_seq, preferred_element_type=jnp.float32)
            * factor
        )
        grad_key = (
            jnp.einsum("hqk,qhd->khd", grad_scores, query_seq, preferred_element_type=jnp.float32)
            * factor
        )
        return (
            grad_query.astype(jnp.bfloat16),
            grad_key.astype(jnp.bfloat16),
            grad_value.astype(jnp.bfloat16),
        )

    head_gq, head_gk, head_gv = lax.map(
        attend_back, (head_q, head_k, head_v, log_total, grad_head_context, lengths)
    )
    tok_gq, tok_gk, tok_gv = (
        lax.all_to_all(head_gq.reshape(back_shape), "seq", split_axis=1, concat_axis=2, tiled=True),
        lax.all_to_all(head_gk.reshape(back_shape), "seq", split_axis=1, concat_axis=2, tiled=True),
        lax.all_to_all(head_gv.reshape(back_shape), "seq", split_axis=1, concat_axis=2, tiled=True),
    )
    grad_query = tok_gq.reshape(-1, model_width)
    grad_key = tok_gk.reshape(-1, model_width)
    grad_value = tok_gv.reshape(-1, model_width)
    grad_w_query = row_contract(flat_rows, grad_query)
    grad_b_query = column_sum(grad_query)
    grad_w_key = row_contract(flat_rows, grad_key)
    grad_w_value = row_contract(flat_rows, grad_value)
    grad_b_value = column_sum(grad_value)
    grad_rows = (
        grad_summed
        + times_transposed(grad_query, query_w)
        + times_transposed(grad_key, key_w)
        + times_transposed(grad_value, value_w)
    )
    local_grads = (
        grad_w_query,
        grad_b_query,
        grad_w_key,
        grad_w_value,
        grad_b_value,
        grad_w_output,
        grad_b_output,
        grad_gain_one,
        grad_shift_one,
        grad_w_inner,
        grad_b_inner,
        grad_w_outer,
        grad_b_outer,
        grad_gain_two,
        grad_shift_two,
    )
    shares = (
        lax.psum_scatter(local_grads[0], "shard", scatter_dimension=0, tiled=True),
        lax.psum_scatter(local_grads[1], "shard", scatter_dimension=0, tiled=True),
        lax.psum_scatter(local_grads[2], "shard", scatter_dimension=0, tiled=True),
        lax.psum_scatter(local_grads[3], "shard", scatter_dimension=0, tiled=True),
        lax.psum_scatter(local_grads[4], "shard", scatter_dimension=0, tiled=True),
        lax.psum_scatter(local_grads[5], "shard", scatter_dimension=0, tiled=True),
        lax.psum_scatter(local_grads[6], "shard", scatter_dimension=0, tiled=True),
        lax.psum_scatter(local_grads[7], "shard", scatter_dimension=0, tiled=True),
        lax.psum_scatter(local_grads[8], "shard", scatter_dimension=0, tiled=True),
        lax.psum_scatter(local_grads[9], "shard", scatter_dimension=0, tiled=True),
        lax.psum_scatter(local_grads[10], "shard", scatter_dimension=0, tiled=True),
        lax.psum_scatter(local_grads[11], "shard", scatter_dimension=0, tiled=True),
        lax.psum_scatter(local_grads[12], "shard", scatter_dimension=0, tiled=True),
        lax.psum_scatter(local_grads[13], "shard", scatter_dimension=0, tiled=True),
        lax.psum_scatter(local_grads[14], "shard", scatter_dimension=0, tiled=True),
    )
    summed_grads = (
        lax.psum(shares[0].astype(jnp.bfloat16), "seq").astype(jnp.float32),
        lax.psum(shares[1].astype(jnp.bfloat16), "seq").astype(jnp.float32),
        lax.psum(shares[2].astype(jnp.bfloat16), "seq").astype(jnp.float32),
        lax.psum(shares[3].astype(jnp.bfloat16), "seq").astype(jnp.float32),
        lax.psum(shares[4].astype(jnp.bfloat16), "seq").astype(jnp.float32),
        lax.psum(shares[5].astype(jnp.bfloat16), "seq").astype(jnp.float32),
        lax.psum(shares[6].astype(jnp.bfloat16), "seq").astype(jnp.float32),
        lax.psum(shares[7].astype(jnp.bfloat16), "seq").astype(jnp.float32),
        lax.psum(shares[8].astype(jnp.bfloat16), "seq").astype(jnp.float32),
        lax.psum(shares[9].astype(jnp.bfloat16), "seq").astype(jnp.float32),
        lax.psum(shares[10].astype(jnp.bfloat16), "seq").astype(jnp.float32),
        lax.psum(shares[11].astype(jnp.bfloat16), "seq").astype(jnp.float32),
        lax.psum(shares[12].astype(jnp.bfloat16), "seq").astype(jnp.float32),
        lax.psum(shares[13].astype(jnp.bfloat16), "seq").astype(jnp.float32),
        lax.psum(shares[14].astype(jnp.bfloat16), "seq").astype(jnp.float32),
    )
    return (
        result.astype(jnp.bfloat16).reshape(shape_seq),
        grad_rows.reshape(shape_seq),
        summed_grads[0],
        summed_grads[1],
        summed_grads[2],
        summed_grads[3],
        summed_grads[4],
        summed_grads[5],
        summed_grads[6],
        summed_grads[7],
        summed_grads[8],
        summed_grads[9],
        summed_grads[10],
        summed_grads[11],
        summed_grads[12],
        summed_grads[13],
        summed_grads[14],
    )


def solution(mesh):
    return jax.shard_map(
        per_device,
        mesh=mesh,
        in_specs=(
            P("shard", "seq", None),
            P("shard"),
            P("shard", None),
            P("shard"),
            P("shard", None),
            P("shard", None),
            P("shard"),
            P("shard", None),
            P("shard"),
            P("shard"),
            P("shard"),
            P("shard", None),
            P("shard"),
            P("shard", None),
            P("shard"),
            P("shard"),
            P("shard"),
            P("shard", "seq", None),
        ),
        out_specs=(
            P("shard", "seq", None),
            P("shard", "seq", None),
            P("shard", None),
            P("shard"),
            P("shard", None),
            P("shard", None),
            P("shard"),
            P("shard", None),
            P("shard"),
            P("shard"),
            P("shard"),
            P("shard", None),
            P("shard"),
            P("shard", None),
            P("shard"),
            P("shard"),
            P("shard"),
        ),
        check_vma=False,
    )
```

profile of v0, /device:TPU:0, one launch (start us, length us, event | category | flops | bytes accessed | tf_op | source)
XLA Modules:
  0.0 1048.1 jit_solution(8084911402475072385)
XLA Ops:
  19.8 39.2 %all-reduce.18 = (bf16[768]{0:T(1024)(128)(2,1)S(1)}, bf16[768]{0:T(1024)(128)(2,1)S(1)}, bf16[768]{0:T(1024)(128)(2,1)S(1)}, bf16[768]{0:T(1024)(128)(2,1)S(1)}...) all-reduce(bf16[768]{0:T(1024)(128)(2,1)S(1)} %dynamic-update-slice, ...), channel_id=1, replica_groups=mesh['shard'=8,'seq'=4] {'shard'}, use_global_device_ids=true, to_apply=%add.1 | all-reduce | flops 6144 | bytes 24576
  59.1 1.9 fusion.62
  62.1 3.5 all-to-all-start
  65.6 30.7 %all-gather.10.cloned.1.call-done = bf16[768,768]{1,0:T(8,128)(2,1)} async-done(((bf16[96,768]{1,0:T(8,128)(2,1)}), bf16[768,768]{1,0:T(8,128)(2,1)}) %all-gather.10.cloned.1.call-update) | async-done | bytes 1179664 | tf_op jit(solution)/shard_map/all_gather | solution.py:72
  99.2 3.5 all-to-all-start.1
  102.6 35.7 %all-gather.12.cloned.1.call-done = bf16[768,768]{1,0:T(8,128)(2,1)} async-done(((bf16[96,768]{1,0:T(8,128)(2,1)}), bf16[768,768]{1,0:T(8,128)(2,1)}) %all-gather.12.cloned.1.call-update) | async-done | bytes 1179664 | tf_op jit(solution)/shard_map/all_gather | solution.py:74
  141.2 3.5 all-to-all-start.2
  145.7 6.3 all-to-all-done.2
  152.6 7.5 while.26
  161.2 3.5 all-to-all-start.3
  164.7 26.5 %all-gather = bf16[8,1,384]{2,1,0:T(2,128)(2,1)S(1)} all-gather(bf16[1,1,384]{2,1,0:T(2,128)(2,1)S(1)} %reshape.251), channel_id=1, replica_groups=mesh['shard'=8,'seq'=4] {'shard'}, dimensions={0}, use_global_device_ids=true | all-gather | bytes 6912 | tf_op jit(solution)/shard_map/all_gather | solution.py:82
  192.7 1.9 fusion.95
  194.9 65.5 %all-gather.16.cloned.1.call-done = bf16[768,3072]{1,0:T(8,128)(2,1)} async-done(((bf16[96,3072]{1,0:T(8,128)(2,1)}), bf16[768,3072]{1,0:T(8,128)(2,1)}) %all-gather.16.cloned.1.call-update) | async-done | bytes 4718608 | tf_op jit(solution)/shard_map/all_gather | solution.py:81
  260.4 12.1 %multiply_convert_fusion.1 = (bf16[256,3072]{1,0:T(8,128)(2,1)}, f32[256,3072]{1,0:T(8,128)}, f32[256,3072]{1,0:T(8,128)}) fusion(f32[3072]{0:T(1024)S(1)} %bitcast.275, bf16[768,3072]{1,0:T(8,128)(2,1)} %all-gather.16.cloned.1.call-done, f32[256,768]{1,0:T(8,128)S(1)} %get-tuple-element.290, f32[768]{0:T(1024)S(1)} %convert_element_type.217, ...), kind=kOutput, calls=%fused_computation.65 | convolution fusion | flops 1260847104 | bytes 13389824 | tf_op jit(solution)/shard_map/dot_general | solution.py:19
  272.4 67.7 %all-gather.18.cloned.1.call-done = bf16[3072,768]{1,0:T(8,128)(2,1)} async-done(((bf16[384,768]{1,0:T(8,128)(2,1)}), bf16[3072,768]{1,0:T(8,128)(2,1)}) %all-gather.18.cloned.1.call-update) | async-done | bytes 4718608 | tf_op jit(solution)/shard_map/all_gather | solution.py:83
  340.1 4.4 fusion.96
  347.2 2.7 convert_reduce_fusion
  349.9 2.3 multiply_reduce_fusion.1
  355.7 3.5 all-to-all-start.4
  359.2 1.9 fusion.75
  361.2 5.4 all-to-all-done.4
  367.9 14.8 %while.27 = (s32[]{:T(128)}, bf16[2,512,3,64]{1,3,2,0:T(8,128)(2,1)S(1)}, bf16[2,512,3,64]{1,3,2,0:T(8,128)(2,1)S(1)}, bf16[2,512,3,64]{1,3,2,0:T(8,128)(2,1)}, ...) while((s32[]{:T(128)}, ...), condition=%wide.region_14.15_spmd, body=%wide.region_12.14_spmd.sunk | while | flops 510884864 | bytes 28743872 | solution.py:197
  383.1 11.4 %all_to_all.120 = bf16[2,512,192]{2,0,1:T(2,128)(2,1)S(1)} all-to-all(bf16[2,512,192]{2,0,1:T(2,128)(2,1)S(1)} %copy.126), channel_id=1, replica_groups=mesh['shard'=8,'seq'=4] {'seq'}, dimensions={1} | all-to-all | bytes 786432 | tf_op jit(solution)/shard_map/all_to_all | solution.py:201
  397.5 2.0 copy.148
  400.9 11.2 %all_to_all.121 = bf16[2,512,192]{2,0,1:T(2,128)(2,1)S(1)} all-to-all(bf16[2,512,192]{2,0,1:T(2,128)(2,1)S(1)} %copy.129), channel_id=1, replica_groups=mesh['shard'=8,'seq'=4] {'seq'}, dimensions={1} | all-to-all | bytes 786432 | tf_op jit(solution)/shard_map/all_to_all | solution.py:202
  414.7 2.0 copy.150
  418.2 11.2 %all_to_all.122 = bf16[2,512,192]{2,0,1:T(2,128)(2,1)S(1)} all-to-all(bf16[2,512,192]{2,0,1:T(2,128)(2,1)S(1)} %copy.132), channel_id=1, replica_groups=mesh['shard'=8,'seq'=4] {'seq'}, dimensions={1} | all-to-all | bytes 786432 | tf_op jit(solution)/shard_map/all_to_all | solution.py:203
  432.3 2.0 copy.152
  435.7 6.4 fusion.88
  443.5 5.1 fusion.97
  451.2 35.5 %all-reduce.17 = (bf16[768]{0:T(1024)(128)(2,1)S(1)}, bf16[768]{0:T(1024)(128)(2,1)S(1)}, bf16[768]{0:T(1024)(128)(2,1)S(1)}, bf16[768]{0:T(1024)(128)(2,1)S(1)}...) all-reduce(f32[768]{0:T(1024)S(1)} %reduce_sum.190, ...), channel_id=3, replica_groups=mesh['shard'=8,'seq'=4] {'shard'}, use_global_device_ids=true, to_apply=%region_18.19.clone | all-reduce | flops 9216 | bytes 55296
  487.4 6.0 all-reduce.19
  499.7 5.1 reduce-scatter.19.cloned.1.call-done
  504.9 1.8 copy.149
  506.6 70.6 %reduce-scatter.21.cloned.1.call-done = f32[96,768]{1,0:T(8,128)} async-done(((f32[768,768]{1,0:T(8,128)}), f32[96,768]{1,0:T(8,128)}) %reduce-scatter.21.cloned.1.call-update) | async-done | bytes 294928
  577.2 1.8 copy.151
  579.0 70.6 %reduce-scatter.23.cloned.1.call-done = f32[96,768]{1,0:T(8,128)} async-done(((f32[768,768]{1,0:T(8,128)}), f32[96,768]{1,0:T(8,128)}) %reduce-scatter.23.cloned.1.call-update) | async-done | bytes 294928
  649.6 1.8 copy.153
  651.4 163.2 %reduce-scatter.15.cloned.1.call-done = f32[96,3072]{1,0:T(8,128)} async-done(((f32[768,3072]{1,0:T(8,128)}), f32[96,3072]{1,0:T(8,128)}) %reduce-scatter.15.cloned.1.call-update) | async-done | bytes 1179664 | tf_op jit(solution)/shard_map/reduce_scatter | solution.py:246
  814.6 2.2 convert_element_type.252
  816.8 162.5 %reduce-scatter.17.cloned.1.call-done = f32[384,768]{1,0:T(8,128)} async-done(((f32[3072,768]{1,0:T(8,128)}), f32[384,768]{1,0:T(8,128)}) %reduce-scatter.17.cloned.1.call-update) | async-done | bytes 1179664 | tf_op jit(solution)/shard_map/reduce_scatter | solution.py:248
  979.3 2.1 convert_element_type.257
  981.5 1.9 convolution_add_fusion.3
  985.4 45.7 %all-reduce.23.cloned.1.call-done = (bf16[96,768]{0,1:T(8,128)(2,1)}, bf16[96,768]{0,1:T(8,128)(2,1)}, bf16[96,768]{0,1:T(8,128)(2,1)}, bf16[96,768]{1,0:T(8,128...) async-done(((bf16[96,768]{0,1:T(8,128)(2,1)}, bf16[96,768]{0,1:T(8,128)(2,1)}, bf16[96,768]{0,1:T(8,128)(2,1)}, bf16[96,768]{1,0:T(8,128)(2,1)}, ...) | async-done | bytes 1769488 | tf_op jit(solution)/shard_map/psum | solution.py:254
  1031.1 1.8 copy.137
  1032.9 1.8 copy.138
  1034.7 1.8 copy.139
  1038.1 2.2 convert_element_type.253
  (267 shorter events, 79.8 us)
Async XLA Ops:
  7.2 89.1 %copy-start.1 = (bf16[2,128,768]{2,1,0:T(8,128)(2,1)S(1)}, bf16[2,128,768]{2,1,0:T(8,128)(2,1)}, u32[]{:S(2)}) copy-start(bf16[2,128,768]{2,1,0:T(8,128)(2,1)} %param.22) | copy-start | bytes 1179652
  7.2 51.9 %all-gather.8.cloned.1.call-start = ((), (), s32[]{:S(2)}) async-start(), calls=%async_computation.14 | async-start | bytes 1327104 | tf_op jit(solution)/shard_map/all_gather | solution.py:75
  7.9 88.4 %all-gather.10.cloned.1.call-start = ((), (), s32[]{:S(2)}) async-start(), calls=%async_computation.15 | async-start | bytes 1327104 | tf_op jit(solution)/shard_map/all_gather | solution.py:72
  8.7 129.7 %all-gather.12.cloned.1.call-start = ((), (), s32[]{:S(2)}) async-start(), calls=%async_computation.16 | async-start | bytes 1327104 | tf_op jit(solution)/shard_map/all_gather | solution.py:74
  9.4 183.3 %all-gather.14.cloned.1.call-start = ((), (), s32[]{:S(2)}) async-start(), calls=%async_computation.17 | async-start | bytes 1327104 | tf_op jit(solution)/shard_map/all_gather | solution.py:77
  10.0 250.4 %all-gather.16.cloned.1.call-start = ((), (), s32[]{:S(2)}) async-start(), calls=%async_computation.18 | async-start | bytes 5308416 | tf_op jit(solution)/shard_map/all_gather | solution.py:81
  10.6 329.6 %all-gather.18.cloned.1.call-start = ((), (), s32[]{:S(2)}) async-start(), calls=%async_computation.19 | async-start | bytes 5308416 | tf_op jit(solution)/shard_map/all_gather | solution.py:83
  62.1 37.1 %all-to-all-start = ((bf16[2,128,768]{1,0,2:T(2,128)(2,1)}), bf16[2,128,768]{1,0,2:T(2,128)(2,1)S(1)}, u32[]{:S(2)}, u32[]{:S(2)}) async-start(bf16[2,128,768]{1,0,2:T(2,128)(2,1)} %copy.111), calls=%async_computation | async-start | bytes 786432 | tf_op jit(solution)/shard_map/all_to_all | solution.py:117
  99.2 42.0 %all-to-all-start.1 = ((bf16[2,128,768]{1,0,2:T(2,128)(2,1)}), bf16[2,128,768]{1,0,2:T(2,128)(2,1)S(1)}, u32[]{:S(2)}, u32[]{:S(2)}) async-start(bf16[2,128,768]{1,0,2:T(2,128)(2,1)} %copy.114), calls=%async_computation.1 | async-start | bytes 786432 | tf_op jit(solution)/shard_map/all_to_all | solution.py:115
  141.2 10.8 %all-to-all-start.2 = ((bf16[2,128,768]{1,0,2:T(2,128)(2,1)}), bf16[2,128,768]{1,0,2:T(2,128)(2,1)S(1)}, u32[]{:S(2)}, u32[]{:S(2)}) async-start(bf16[2,128,768]{1,0,2:T(2,128)(2,1)} %copy.117), calls=%async_computation.2 | async-start | bytes 786432 | tf_op jit(solution)/shard_map/all_to_all | solution.py:116
  145.0 7.6 copy-start.37
  152.6 12.1 %copy-start.36 = (bf16[384]{0:T(512)(128)(2,1)S(1)}, bf16[384]{0:T(512)(128)(2,1)}, u32[]{:S(2)}) copy-start(bf16[384]{0:T(512)(128)(2,1)} %param.34) | copy-start | bytes 2308
  160.1 32.2 %copy-start.26 = (f32[2,3,512]{2,1,0:T(4,128)}, f32[2,3,512]{2,1,0:T(4,128)S(1)}, u32[]{:S(2)}) copy-start(f32[2,3,512]{2,1,0:T(4,128)S(1)} %get-tuple-element.438) | copy-start | bytes 36868
  161.2 30.1 %all-to-all-start.3 = ((bf16[2,512,192]{2,0,1:T(2,128)(2,1)}), bf16[2,512,192]{2,0,1:T(2,128)(2,1)S(1)}, u32[]{:S(2)}, u32[]{:S(2)}) async-start(bf16[2,512,192]{2,0,1:T(2,128)(2,1)} %copy.120), calls=%async_computation.3 | async-start | bytes 1048576 | tf_op jit(solution)/shard_map/all_to_all | solution.py:137
  194.6 157.6 %copy-start = (f32[256,768]{1,0:T(8,128)}, f32[256,768]{1,0:T(8,128)S(1)}, u32[]{:S(2)}) copy-start(f32[256,768]{1,0:T(8,128)S(1)} %get-tuple-element.290) | copy-start | bytes 2359300
  194.8 155.1 %copy-start.29 = (f32[256]{0:T(256)}, f32[256]{0:T(256)S(1)}, u32[]{:S(2)}) copy-start(f32[256]{0:T(256)S(1)} %fusion.86) | copy-start | bytes 3076
  340.1 7.0 slice-start.2
  340.1 4.7 copy-start.7
  340.1 7.0 slice-start.3
  340.1 7.0 copy-start.39
  344.6 2.6 copy-start.38
  346.4 3.5 slice-start
  347.1 2.8 copy-start.16
  347.2 2.8 slice-start.1
  349.9 2.3 copy-start.21
  355.7 10.8 %all-to-all-start.4 = ((bf16[2,128,768]{1,0,2:T(2,128)(2,1)}), bf16[2,128,768]{1,0,2:T(2,128)(2,1)S(1)}, u32[]{:S(2)}, u32[]{:S(2)}) async-start(bf16[2,128,768]{1,0,2:T(2,128)(2,1)} %copy.123), calls=%async_computation.4 | async-start | bytes 786432 | tf_op jit(solution)/shard_map/all_to_all | solution.py:166
  359.2 138.9 %reduce-scatter.13.cloned.1.call-start = ((), (), s32[]{:S(2)}) async-start(), calls=%async_computation.20 | async-start | bytes 2654208 | tf_op jit(solution)/shard_map/reduce_scatter | solution.py:242
  361.1 143.7 %reduce-scatter.19.cloned.1.call-start = ((), (), s32[]{:S(2)}) async-start(), calls=%async_computation.23 | async-start | bytes 2654208
  382.7 13.2 %copy-start.18 = (bf16[2,512,3,64]{1,3,2,0:T(8,128)(2,1)}, bf16[2,512,3,64]{1,3,2,0:T(8,128)(2,1)S(1)}, u32[]{:S(2)}) copy-start(bf16[2,512,3,64]{1,3,2,0:T(8,128)(2,1)S(1)} %get-tuple-element.112) | copy-start | bytes 1179652
  399.5 177.7 %reduce-scatter.21.cloned.1.call-start = ((), (), s32[]{:S(2)}) async-start(), calls=%async_computation.24 | async-start | bytes 2654208
  416.8 232.8 %reduce-scatter.23.cloned.1.call-start = ((), (), s32[]{:S(2)}) async-start(), calls=%async_computation.25 | async-start | bytes 2654208
  432.3 2.0 copy-start.30
  434.3 380.3 %reduce-scatter.15.cloned.1.call-start = ((), (), s32[]{:S(2)}) async-start(), calls=%async_computation.21 | async-start | bytes 10616832 | tf_op jit(solution)/shard_map/reduce_scatter | solution.py:246
  442.1 537.2 %reduce-scatter.17.cloned.1.call-start = ((), (), s32[]{:S(2)}) async-start(), calls=%async_computation.22 | async-start | bytes 10616832 | tf_op jit(solution)/shard_map/reduce_scatter | solution.py:248
  448.6 2.0 copy-start.12
  448.6 2.5 copy-start.27
  448.6 2.5 copy-start.28
  448.6 2.5 copy-start.31
  448.7 2.5 copy-start.34
  448.7 2.5 copy-start.35
  448.7 582.4 %all-reduce.23.cloned.1.call-start = ((), (), s32[]{:S(2)}) async-start(), calls=%async_computation.26 | async-start | bytes 3833856 | tf_op jit(solution)/shard_map/psum | solution.py:254
  506.6 474.8 %copy-start.14 = (bf16[2,128,4,192]{1,0,3,2:T(2,128)(2,1)S(1)}, bf16[2,128,4,192]{1,0,3,2:T(2,128)(2,1)}, u32[]{:S(2)}) copy-start(bf16[2,128,4,192]{1,0,3,2:T(2,128)(2,1)} %copy-done.13) | copy-start | bytes 1179652
  506.6 474.8 %copy-start.33 = (f32[256]{0:T(256)S(1)}, f32[256]{0:T(256)}, u32[]{:S(2)}) copy-start(f32[256]{0:T(256)} %copy-done.32) | copy-start | bytes 3076
  816.8 166.7 %copy-start.2 = (bf16[768,768]{1,0:T(8,128)(2,1)S(1)}, bf16[768,768]{1,0:T(8,128)(2,1)}, u32[]{:S(2)}) copy-start(bf16[768,768]{1,0:T(8,128)(2,1)} %all-gather.12.cloned.1.call-done) | copy-start | bytes 3538948
  816.8 166.7 %copy-start.4 = (bf16[2,128,4,192]{1,0,3,2:T(2,128)(2,1)S(1)}, bf16[2,128,4,192]{1,0,3,2:T(2,128)(2,1)}, u32[]{:S(2)}) copy-start(bf16[2,128,4,192]{1,0,3,2:T(2,128)(2,1)} %copy-done.3) | copy-start | bytes 1179652
  981.5 2.5 copy-start.6
  981.5 2.5 copy-start.23
  1031.1 9.2 copy-start.25
  (16 other events, 17.3 us)
Sparse Core Ops, SparseCore 0:
  10.2 44.0 all-gather.7
  56.5 39.7 all-gather.9
  98.5 39.8 all-gather.11
  140.4 39.8 all-gather.13
  182.3 78.0 all-gather.15
  262.4 77.6 all-gather.17
  363.5 68.4 reduce-scatter.12
  435.5 69.3 reduce-scatter.18
  508.4 68.8 reduce-scatter.20
  580.6 68.9 reduce-scatter.22
  653.2 161.3 reduce-scatter.14
  818.0 161.1 reduce-scatter.16
  983.2 47.7 all-reduce.22
where the time goes:
time: 1060 us; the launch traced here: 1050 us
  waiting for transfers between devices  733 us (69%)
  blocking collectives  141 us (13%)
  matrix products  57.6 us (5%)
  local copies, waits for them, and re-layouts  55 us (5%)
  other arithmetic  26.5 us (2%)
  starting transfers between devices  17.8 us (2%)
  between operations  17 us (2%)
    reduce_scatter x1, waiting for transfers between devices, per_device(): lax.psum_scatter(local_grads[9], 'shard', scatter_dimension=0, tiled=True)  163 us
    reduce_scatter x1, waiting for transfers between devices, per_device(): lax.psum_scatter(local_grads[11], 'shard', scatter_dimension=0, tiled=True)  163 us
    unnamed x16, waiting for transfers between devices  150 us
    unnamed x2, blocking collectives  74.8 us
    all_gather x1, waiting for transfers between devices, per_device(): lax.all_gather(w_outer, 'shard', axis=0, tiled=True)  67.7 us
    all_gather x1, waiting for transfers between devices, per_device(): lax.all_gather(w_inner, 'shard', axis=0, tiled=True)  65.5 us
    psum x1, waiting for transfers between devices, per_device(): lax.psum(shares[0].astype(jnp.bfloat16), 'seq').astype(jnp.float32)  45.7 us
    all_gather x1, waiting for transfers between devices, per_device(): lax.all_gather(w_key, 'shard', axis=0, tiled=True)  35.7 us
  transfers between devices with their start and end apart: 18, of which 12 were waited for; matrix products, arithmetic and copies ran while one was open for 10% of the time, Pallas kernels for 0%

commit v1 on v0

--- a/solution.py
+++ b/solution.py
@@ -6,6 +6,35 @@
 
 HEAD_DIM = 64
 epsilon = 1e-12
+
+
+def files_apply(incoming_x):
+    response, answer, low = (
+        jax.lax.psum(1, "shard"),
+        jax.lax.axis_index("shard"),
+        incoming_x.shape[0],
+    )
+    items = list(map(lambda hop_no: (hop_no, (hop_no + 1) % response), range(response)))
+    queue = list(map(lambda hop_no: (hop_no, (hop_no - 1) % response), range(response)))
+    e_next = jnp.zeros(
+        (*incoming_x.shape[:0], response * low, *incoming_x.shape[1:]), incoming_x.dtype
+    )
+    e_next = lax.dynamic_update_slice_in_dim(e_next, incoming_x, answer * low, axis=0)
+    kept_arr = arr_now = incoming_x
+    x_now = response // 2
+    p = 1
+    while p < x_now + 1:
+        kept_arr = jax.lax.ppermute(kept_arr, "shard", items)
+        e_next = lax.dynamic_update_slice_in_dim(
+            e_next, kept_arr, (answer - p) % response * low, axis=0
+        )
+        if p < response - x_now:
+            arr_now = jax.lax.ppermute(arr_now, "shard", queue)
+            e_next = lax.dynamic_update_slice_in_dim(
+                e_next, arr_now, (answer + p) % response * low, axis=0
+            )
+        p = p + 1
+    return e_next
 
 
 def layer_norm(tensor, norm_gain, norm_shift):
@@ -69,7 +98,7 @@
     local_heads = head_width // HEAD_DIM
     factor = HEAD_DIM ** (-0.5)
     gathered = (
-        lax.all_gather(w_query, "shard", axis=0, tiled=True),
+        files_apply(w_query),
         lax.all_gather(b_query, "shard", axis=0, tiled=True),
         lax.all_gather(w_key, "shard", axis=0, tiled=True),
         lax.all_gather(w_value, "shard", axis=0, tiled=True),

time: 1060 us -> 1020 us (0.962)
  waiting for transfers between devices: 733 us -> 671 us
  starting transfers between devices: 17.8 us -> 34.5 us
    all_gather x1, waiting for transfers between devices: 35.7 us -> 0.02 us  [per_device(): lax.all_gather(w_key, 'shard', axis=0, tiled=True)]
    all_gather x1 -> x0, waiting for transfers between devices: 30.7 us -> none  [per_device(): lax.all_gather(w_query, 'shard', axis=0, tiled=True)]
    all_gather x1, waiting for transfers between devices: 65.5 us -> 47.4 us  [per_device(): lax.all_gather(w_inner, 'shard', axis=0, tiled=True)]
    ppermute x0 -> x7, starting transfers between devices: none -> 16.7 us  [the longest x3 11.3 us: files_apply(): arr_now = jax.lax.ppermute(arr_now, 'shard', queue)]
    ppermute x0 -> x7, waiting for transfers between devices: none -> 14.3 us  [the longest x4 14.2 us: files_apply(): kept_arr = jax.lax.ppermute(kept_arr, 'shard', items)]
    all_gather x1, blocking collectives: 26.5 us -> 38.6 us  [per_device(): lax.all_gather(b_inner, 'shard', axis=0, tiled=True)]
    unnamed x120 -> x130, local copies, waits for them, and re-layouts: 31.2 us -> 29.4 us
    unnamed x16 -> x15, waiting for transfers between devices: 150 us -> 149 us
  transfers between devices with their start and end apart: 18 -> 24, of which waited for: 12 -> 16; matrix products, arithmetic and copies ran while one was open for 10% -> 10% of each run, Pallas kernels for 0% -> 0%
where the time goes in v1:
time: 1020 us; the launch traced here: 1010 us
  waiting for transfers between devices  671 us (66%)
  blocking collectives  149 us (15%)
  matrix products  56.9 us (6%)
  local copies, waits for them, and re-layouts  52 us (5%)
  starting transfers between devices  34.5 us (3%)
  other arithmetic  26.7 us (3%)
  between operations  17.8 us (2%)
    reduce_scatter x1, waiting for transfers between devices, per_device(): lax.psum_scatter(local_grads[9], 'shard', scatter_dimension=0, tiled=True)  163 us
    reduce_scatter x1, waiting for transfers between devices, per_device(): lax.psum_scatter(local_grads[11], 'shard', scatter_dimension=0, tiled=True)  163 us
    unnamed x15, waiting for transfers between devices  149 us
    unnamed x2, blocking collectives  70.4 us
    all_gather x1, waiting for transfers between devices, per_device(): lax.all_gather(w_outer, 'shard', axis=0, tiled=True)  68.1 us
    all_gather x1, waiting for transfers between devices, per_device(): lax.all_gather(w_inner, 'shard', axis=0, tiled=True)  47.4 us
    psum x1, waiting for transfers between devices, per_device(): lax.psum(shares[0].astype(jnp.bfloat16), 'seq').astype(jnp.float32)  45.8 us
    all_gather x1, blocking collectives, per_device(): lax.all_gather(b_inner, 'shard', axis=0, tiled=True)  38.6 us
  transfers between devices with their start and end apart: 24, of which 16 were waited for; matrix products, arithmetic and copies ran while one was open for 10% of the time, Pallas kernels for 0%

profile of v1, /device:TPU:0, one launch (start us, length us, event | category | flops | bytes accessed | tf_op | source)
XLA Modules:
  0.0 1007.8 jit_solution(11591582794456072031)
XLA Ops:
  10.0 3.0 collective-permute-start
  13.1 3.1 collective-permute-start.1
  25.0 35.0 %all-reduce.18 = (bf16[768]{0:T(1024)(128)(2,1)S(1)}, bf16[768]{0:T(1024)(128)(2,1)S(1)}, bf16[768]{0:T(1024)(128)(2,1)S(1)}, bf16[768]{0:T(1024)(128)(2,1)S(1)}...) all-reduce(bf16[768]{0:T(1024)(128)(2,1)S(1)} %dynamic-update-slice, ...), channel_id=1, replica_groups=mesh['shard'=8,'seq'=4] {'shard'}, use_global_device_ids=true, to_apply=%add.1 | all-reduce | flops 6144 | bytes 24576
  60.2 4.7 collective-permute-start.3
  65.0 3.2 collective-permute-done.2
  68.2 2.0 collective-permute-start.4
  70.2 3.5 collective-permute-start.5
  73.7 3.6 collective-permute-done.4
  77.7 7.4 collective-permute-done.6
  87.8 3.5 all-to-all-start.1
  94.1 4.5 all-to-all-done.1
  98.6 3.5 all-to-all-start
  105.0 4.5 all-to-all-done
  109.5 3.5 all-to-all-start.2
  114.0 6.3 all-to-all-done.2
  120.9 7.5 while.26
  129.5 3.5 all-to-all-start.3
  133.0 38.6 %all-gather = bf16[8,1,384]{2,1,0:T(2,128)(2,1)S(1)} all-gather(bf16[1,1,384]{2,1,0:T(2,128)(2,1)S(1)} %reshape.251), channel_id=1, replica_groups=mesh['shard'=8,'seq'=4] {'shard'}, dimensions={0}, use_global_device_ids=true | all-gather | bytes 6912 | tf_op jit(solution)/shard_map/all_gather | solution.py:111
  175.3 47.4 %all-gather.13.cloned.1.call-done = bf16[768,3072]{1,0:T(8,128)(2,1)} async-done(((bf16[96,3072]{1,0:T(8,128)(2,1)}), bf16[768,3072]{1,0:T(8,128)(2,1)}) %all-gather.13.cloned.1.call-update) | async-done | bytes 4718608 | tf_op jit(solution)/shard_map/all_gather | solution.py:110
  222.7 11.7 %multiply_convert_fusion.1 = (bf16[256,3072]{1,0:T(8,128)(2,1)}, f32[256,3072]{1,0:T(8,128)}, f32[256,3072]{1,0:T(8,128)}) fusion(f32[3072]{0:T(1024)S(1)} %bitcast.276, bf16[768,3072]{1,0:T(8,128)(2,1)} %all-gather.13.cloned.1.call-done, f32[256,768]{1,0:T(8,128)S(1)} %get-tuple-element.290, f32[768]{0:T(1024)S(1)} %convert_element_type.221, ...), kind=kOutput, calls=%fused_computation.65 | convolution fusion | flops 1260847104 | bytes 13389824 | tf_op jit(solution)/shard_map/dot_general | solution.py:48
  234.3 68.1 %all-gather.15.cloned.1.call-done = bf16[3072,768]{1,0:T(8,128)(2,1)} async-done(((bf16[384,768]{1,0:T(8,128)(2,1)}), bf16[3072,768]{1,0:T(8,128)(2,1)}) %all-gather.15.cloned.1.call-update) | async-done | bytes 4718608 | tf_op jit(solution)/shard_map/all_gather | solution.py:112
  302.4 4.4 fusion.98
  309.4 2.7 convert_reduce_fusion
  312.2 2.3 multiply_reduce_fusion.1
  318.0 3.5 all-to-all-start.4
  321.5 1.9 fusion.77
  323.4 5.4 all-to-all-done.4
  330.2 14.6 %while.27 = (s32[]{:T(128)}, bf16[2,512,3,64]{1,3,2,0:T(8,128)(2,1)S(1)}, bf16[2,512,3,64]{1,3,2,0:T(8,128)(2,1)S(1)}, bf16[2,512,3,64]{1,3,2,0:T(8,128)(2,1)}, ...) while((s32[]{:T(128)}, ...), condition=%wide.region_14.15_spmd, body=%wide.region_12.14_spmd.sunk | while | flops 510884864 | bytes 25598080 | solution.py:226
  345.2 11.2 %all_to_all.120 = bf16[2,512,192]{2,0,1:T(2,128)(2,1)S(1)} all-to-all(bf16[2,512,192]{2,0,1:T(2,128)(2,1)S(1)} %copy.126), channel_id=1, replica_groups=mesh['shard'=8,'seq'=4] {'seq'}, dimensions={1} | all-to-all | bytes 786432 | tf_op jit(solution)/shard_map/all_to_all | solution.py:230
  359.4 2.0 copy.148
  362.8 11.2 %all_to_all.121 = bf16[2,512,192]{2,0,1:T(2,128)(2,1)S(1)} all-to-all(bf16[2,512,192]{2,0,1:T(2,128)(2,1)S(1)} %copy.129), channel_id=1, replica_groups=mesh['shard'=8,'seq'=4] {'seq'}, dimensions={1} | all-to-all | bytes 786432 | tf_op jit(solution)/shard_map/all_to_all | solution.py:231
  376.7 2.0 copy.150
  380.1 11.2 %all_to_all.122 = bf16[2,512,192]{2,0,1:T(2,128)(2,1)S(1)} all-to-all(bf16[2,512,192]{2,0,1:T(2,128)(2,1)S(1)} %copy.132), channel_id=1, replica_groups=mesh['shard'=8,'seq'=4] {'seq'}, dimensions={1} | all-to-all | bytes 786432 | tf_op jit(solution)/shard_map/all_to_all | solution.py:232
  394.3 2.0 copy.152
  397.7 6.3 fusion.90
  405.5 5.1 fusion.99
  413.1 35.4 %all-reduce.17 = (bf16[768]{0:T(1024)(128)(2,1)S(1)}, bf16[768]{0:T(1024)(128)(2,1)S(1)}, bf16[768]{0:T(1024)(128)(2,1)S(1)}, bf16[768]{0:T(1024)(128)(2,1)S(1)}...) all-reduce(f32[768]{0:T(1024)S(1)} %reduce_sum.190, ...), channel_id=3, replica_groups=mesh['shard'=8,'seq'=4] {'shard'}, use_global_device_ids=true, to_apply=%region_18.19.clone | all-reduce | flops 9216 | bytes 55296
  449.1 6.4 all-reduce.19
  461.8 4.9 reduce-scatter.19.cloned.1.call-done
  468.5 70.6 %reduce-scatter.21.cloned.1.call-done = f32[96,768]{1,0:T(8,128)} async-done(((f32[768,768]{1,0:T(8,128)}), f32[96,768]{1,0:T(8,128)}) %reduce-scatter.21.cloned.1.call-update) | async-done | bytes 294928
  540.9 70.6 %reduce-scatter.23.cloned.1.call-done = f32[96,768]{1,0:T(8,128)} async-done(((f32[768,768]{1,0:T(8,128)}), f32[96,768]{1,0:T(8,128)}) %reduce-scatter.23.cloned.1.call-update) | async-done | bytes 294928
  613.3 163.0 %reduce-scatter.15.cloned.1.call-done = f32[96,3072]{1,0:T(8,128)} async-done(((f32[768,3072]{1,0:T(8,128)}), f32[96,3072]{1,0:T(8,128)}) %reduce-scatter.15.cloned.1.call-update) | async-done | bytes 1179664 | tf_op jit(solution)/shard_map/reduce_scatter | solution.py:275
  776.3 2.2 convert_element_type.256
  778.5 162.7 %reduce-scatter.17.cloned.1.call-done = f32[384,768]{1,0:T(8,128)} async-done(((f32[3072,768]{1,0:T(8,128)}), f32[384,768]{1,0:T(8,128)}) %reduce-scatter.17.cloned.1.call-update) | async-done | bytes 1179664 | tf_op jit(solution)/shard_map/reduce_scatter | solution.py:277
  941.1 2.2 convert_element_type.261
  947.0 45.8 %all-reduce.23.cloned.1.call-done = (bf16[96,768]{0,1:T(8,128)(2,1)}, bf16[96,768]{0,1:T(8,128)(2,1)}, bf16[96,768]{0,1:T(8,128)(2,1)}, bf16[96,768]{1,0:T(8,128...) async-done(((bf16[96,768]{0,1:T(8,128)(2,1)}, bf16[96,768]{0,1:T(8,128)(2,1)}, bf16[96,768]{0,1:T(8,128)(2,1)}, bf16[96,768]{1,0:T(8,128)(2,1)}, ...) | async-done | bytes 1769488 | tf_op jit(solution)/shard_map/psum | solution.py:283
  992.8 2.2 convert_element_type.257
  995.0 2.2 convert_element_type.262
  (289 shorter events, 90.3 us)
Async XLA Ops:
  7.2 52.9 %copy-start.28 = (bf16[96,768]{1,0:T(8,128)(2,1)S(1)}, bf16[96,768]{1,0:T(8,128)(2,1)}, u32[]{:S(2)}) copy-start(bf16[96,768]{1,0:T(8,128)(2,1)} %param.24) | copy-start | bytes 442372
  7.2 79.0 %copy-start.1 = (bf16[2,128,768]{2,1,0:T(8,128)(2,1)S(1)}, bf16[2,128,768]{2,1,0:T(8,128)(2,1)}, u32[]{:S(2)}) copy-start(bf16[2,128,768]{2,1,0:T(8,128)(2,1)} %param.22) | copy-start | bytes 1179652
  7.2 84.1 %all-gather.7.cloned.1.call-start = ((), (), s32[]{:S(2)}) async-start(), calls=%async_computation.14 | async-start | bytes 1327104 | tf_op jit(solution)/shard_map/all_gather | solution.py:104
  7.9 94.2 %all-gather.9.cloned.1.call-start = ((), (), s32[]{:S(2)}) async-start(), calls=%async_computation.15 | async-start | bytes 1327104 | tf_op jit(solution)/shard_map/all_gather | solution.py:103
  8.7 164.5 %all-gather.11.cloned.1.call-start = ((), (), s32[]{:S(2)}) async-start(), calls=%async_computation.16 | async-start | bytes 1327104 | tf_op jit(solution)/shard_map/all_gather | solution.py:106
  9.4 213.2 %all-gather.13.cloned.1.call-start = ((), (), s32[]{:S(2)}) async-start(), calls=%async_computation.17 | async-start | bytes 5308416 | tf_op jit(solution)/shard_map/all_gather | solution.py:110
  10.0 292.4 %all-gather.15.cloned.1.call-start = ((), (), s32[]{:S(2)}) async-start(), calls=%async_computation.18 | async-start | bytes 5308416 | tf_op jit(solution)/shard_map/all_gather | solution.py:112
  10.0 50.1 %collective-permute-start = (bf16[96,768]{1,0:T(8,128)(2,1)}, bf16[96,768]{1,0:T(8,128)(2,1)S(1)}, u32[]{:S(2)}, u32[]{:S(2)}) collective-permute-start(bf16[96,768]{1,0:T(8,128)(2,1)} %param.24), channel_id=1, source_target_pairs={{0,4},{4,8},{8,12},{12,16},{16,20},{20,24},{24,28},{28,0},{1,5},{5... | collective-permute-start | bytes 442376 | tf_op jit(solution)/shard_map/ppermute | solution.py:27
  13.1 47.2 %collective-permute-start.1 = (bf16[96,768]{1,0:T(8,128)(2,1)}, bf16[96,768]{1,0:T(8,128)(2,1)S(1)}, u32[]{:S(2)}, u32[]{:S(2)}) collective-permute-start(bf16[96,768]{1,0:T(8,128)(2,1)} %param.24), channel_id=1, source_target_pairs={{0,28},{4,0},{8,4},{12,8},{16,12},{20,16},{24,20},{28,24},{1,29},{... | collective-permute-start | bytes 442376 | tf_op jit(solution)/shard_map/ppermute | solution.py:32
  60.2 8.0 collective-permute-start.2
  60.2 9.9 collective-permute-start.3
  68.2 9.1 collective-permute-start.4
  70.2 7.6 collective-permute-start.5
  77.3 7.8 collective-permute-start.6
  87.8 10.8 %all-to-all-start.1 = ((bf16[2,128,768]{1,0,2:T(2,128)(2,1)}), bf16[2,128,768]{1,0,2:T(2,128)(2,1)S(1)}, u32[]{:S(2)}, u32[]{:S(2)}) async-start(bf16[2,128,768]{1,0,2:T(2,128)(2,1)} %copy.114), calls=%async_computation.1 | async-start | bytes 786432 | tf_op jit(solution)/shard_map/all_to_all | solution.py:144
  98.6 10.8 %all-to-all-start = ((bf16[2,128,768]{1,0,2:T(2,128)(2,1)}), bf16[2,128,768]{1,0,2:T(2,128)(2,1)S(1)}, u32[]{:S(2)}, u32[]{:S(2)}) async-start(bf16[2,128,768]{1,0,2:T(2,128)(2,1)} %copy.111), calls=%async_computation | async-start | bytes 786432 | tf_op jit(solution)/shard_map/all_to_all | solution.py:146
  109.5 10.8 %all-to-all-start.2 = ((bf16[2,128,768]{1,0,2:T(2,128)(2,1)}), bf16[2,128,768]{1,0,2:T(2,128)(2,1)S(1)}, u32[]{:S(2)}, u32[]{:S(2)}) async-start(bf16[2,128,768]{1,0,2:T(2,128)(2,1)} %copy.117), calls=%async_computation.2 | async-start | bytes 786432 | tf_op jit(solution)/shard_map/all_to_all | solution.py:145
  113.3 7.6 copy-start.40
  120.9 12.1 %copy-start.39 = (bf16[384]{0:T(512)(128)(2,1)S(1)}, bf16[384]{0:T(512)(128)(2,1)}, u32[]{:S(2)}) copy-start(bf16[384]{0:T(512)(128)(2,1)} %param.34) | copy-start | bytes 2308
  128.4 43.3 %copy-start.29 = (f32[2,3,512]{2,1,0:T(4,128)}, f32[2,3,512]{2,1,0:T(4,128)S(1)}, u32[]{:S(2)}) copy-start(f32[2,3,512]{2,1,0:T(4,128)S(1)} %get-tuple-element.438) | copy-start | bytes 36868
  129.5 42.2 %all-to-all-start.3 = ((bf16[2,512,192]{2,0,1:T(2,128)(2,1)}), bf16[2,512,192]{2,0,1:T(2,128)(2,1)S(1)}, u32[]{:S(2)}, u32[]{:S(2)}) async-start(bf16[2,512,192]{2,0,1:T(2,128)(2,1)} %copy.120), calls=%async_computation.3 | async-start | bytes 1048576 | tf_op jit(solution)/shard_map/all_to_all | solution.py:166
  175.0 139.5 %copy-start = (f32[256,768]{1,0:T(8,128)}, f32[256,768]{1,0:T(8,128)S(1)}, u32[]{:S(2)}) copy-start(f32[256,768]{1,0:T(8,128)S(1)} %get-tuple-element.290) | copy-start | bytes 2359300
  175.3 136.9 %copy-start.32 = (f32[256]{0:T(256)}, f32[256]{0:T(256)S(1)}, u32[]{:S(2)}) copy-start(f32[256]{0:T(256)S(1)} %fusion.88) | copy-start | bytes 3076
  302.4 7.0 slice-start.2
  302.4 4.7 copy-start.10
  302.4 7.0 slice-start.3
  302.4 7.0 copy-start.42
  306.9 2.6 copy-start.41
  308.7 3.5 slice-start
  309.4 2.8 copy-start.17
  309.4 2.8 slice-start.1
  318.0 10.8 %all-to-all-start.4 = ((bf16[2,128,768]{1,0,2:T(2,128)(2,1)}), bf16[2,128,768]{1,0,2:T(2,128)(2,1)S(1)}, u32[]{:S(2)}, u32[]{:S(2)}) async-start(bf16[2,128,768]{1,0,2:T(2,128)(2,1)} %copy.123), calls=%async_computation.4 | async-start | bytes 786432 | tf_op jit(solution)/shard_map/all_to_all | solution.py:195
  321.4 138.8 %reduce-scatter.13.cloned.1.call-start = ((), (), s32[]{:S(2)}) async-start(), calls=%async_computation.19 | async-start | bytes 2654208 | tf_op jit(solution)/shard_map/reduce_scatter | solution.py:271
  323.4 143.4 %reduce-scatter.19.cloned.1.call-start = ((), (), s32[]{:S(2)}) async-start(), calls=%async_computation.22 | async-start | bytes 2654208
  344.8 13.1 %copy-start.19 = (bf16[2,512,3,64]{1,3,2,0:T(8,128)(2,1)}, bf16[2,512,3,64]{1,3,2,0:T(8,128)(2,1)S(1)}, u32[]{:S(2)}) copy-start(bf16[2,512,3,64]{1,3,2,0:T(8,128)(2,1)S(1)} %get-tuple-element.112) | copy-start | bytes 1179652
  361.5 177.7 %reduce-scatter.21.cloned.1.call-start = ((), (), s32[]{:S(2)}) async-start(), calls=%async_computation.23 | async-start | bytes 2654208
  378.7 232.8 %reduce-scatter.23.cloned.1.call-start = ((), (), s32[]{:S(2)}) async-start(), calls=%async_computation.24 | async-start | bytes 2654208
  396.3 380.0 %reduce-scatter.15.cloned.1.call-start = ((), (), s32[]{:S(2)}) async-start(), calls=%async_computation.20 | async-start | bytes 10616832 | tf_op jit(solution)/shard_map/reduce_scatter | solution.py:275
  404.0 537.1 %reduce-scatter.17.cloned.1.call-start = ((), (), s32[]{:S(2)}) async-start(), calls=%async_computation.21 | async-start | bytes 10616832 | tf_op jit(solution)/shard_map/reduce_scatter | solution.py:277
  410.6 582.1 %all-reduce.23.cloned.1.call-start = ((), (), s32[]{:S(2)}) async-start(), calls=%async_computation.25 | async-start | bytes 3833856 | tf_op jit(solution)/shard_map/psum | solution.py:283
  468.5 474.8 %copy-start.2 = (bf16[768,768]{1,0:T(8,128)(2,1)S(1)}, bf16[768,768]{1,0:T(8,128)(2,1)}, u32[]{:S(2)}) copy-start(bf16[768,768]{1,0:T(8,128)(2,1)} %all-gather.9.cloned.1.call-done) | copy-start | bytes 3538948
  778.4 166.5 %copy-start.4 = (bf16[768,768]{1,0:T(8,128)(2,1)S(1)}, bf16[768,768]{1,0:T(8,128)(2,1)}, u32[]{:S(2)}) copy-start(bf16[768,768]{1,0:T(8,128)(2,1)} %copy-done.3) | copy-start | bytes 3538948
  778.4 166.5 %copy-start.6 = (bf16[2,128,4,192]{1,0,3,2:T(2,128)(2,1)S(1)}, bf16[2,128,4,192]{1,0,3,2:T(2,128)(2,1)}, u32[]{:S(2)}) copy-start(bf16[2,128,4,192]{1,0,3,2:T(2,128)(2,1)} %copy-done.5) | copy-start | bytes 1179652
  778.5 166.5 %copy-start.36 = (f32[256]{0:T(256)S(1)}, f32[256]{0:T(256)}, u32[]{:S(2)}) copy-start(f32[256]{0:T(256)} %copy-done.35) | copy-start | bytes 3076
  992.8 4.4 copy-start.27
  992.8 5.1 copy-start.26
  992.8 6.0 copy-start.25
  992.8 6.9 copy-start.24
  (23 other events, 38.1 us)
Sparse Core Ops, SparseCore 0:
  10.2 43.8 all-gather.6
  56.3 44.0 all-gather.8
  102.6 39.7 all-gather.10
  144.5 78.1 all-gather.12
  224.7 77.6 all-gather.14
  325.4 68.4 reduce-scatter.12
  397.4 69.3 reduce-scatter.18
  470.2 68.8 reduce-scatter.20
  542.6 68.8 reduce-scatter.22
  614.9 161.3 reduce-scatter.14
  779.9 161.1 reduce-scatter.16
  944.9 47.7 all-reduce.22
